TPU v7x, 32 devices: a whole 2x2x4 slice. The times are simulated.
32 devices in a mesh: row: 4 (over y, core), col: 2 (over x), depth: 4 (over z).
Axes of the slice: x: 2, y: 2, z: 4, core: 2. Of those that a mesh axis runs over, the one named last changes fastest.
Arguments:
- density: float32 [512, 5, 128, 128], P(('row', 'depth'), None, 'col'), may hold values from -0.6 to 0.6
- pattern: int32 [512, 5], P(('row', 'depth')), may hold values 0 or 1
Outputs:
- purified: float32 [512, 5, 128, 128], P(('row', 'depth'), None, 'col')
All inputs are finite; a program needn't handle non-finite values. No bound on the sum of `pattern` on one device may be relied on, other than what follows from the above.
Results may differ from a plain program's by a relative error of at most 0.0001.
Values sent between devices are 32-bit elements; how exact they have to be, the bound alone decides.
A program may use at most 64 MiB of HBM per device.

v0:
```python
import jax
import jax.numpy as jnp
from jax import lax
from jax.sharding import PartitionSpec as P

HALF = 2
WIDE = 5


def with_halo(cells, sides, width):
    for axis, dim in sides:
        count = lax.axis_size(axis)
        head = lax.slice_in_dim(cells, 0, width, axis=dim)
        tail = lax.slice_in_dim(cells, cells.shape[dim] - width, cells.shape[dim], axis=dim)
        cells = jnp.concatenate(
            [
                lax.ppermute(tail, axis, [(i, (i + 1) % count) for i in range(count)]),
                cells,
                lax.ppermute(head, axis, [((i + 1) % count, i) for i in range(count)]),
            ],
            axis=dim,
        )
    return cells


def banded_local(left_tiles, extended, pattern):
    rows_here = left_tiles.shape[0]
    summed = jnp.zeros(left_tiles.shape, jnp.float32)
    for source in range(WIDE):
        first_slot = max(0, source - HALF)
        last_slot = min(WIDE, source + HALF + 1)
        partner = extended[
            source : source + rows_here, first_slot - source + HALF : last_slot - source + HALF
        ]
        contrib = jnp.einsum(
            "iab,itbc->itac", left_tiles[:, source], partner, precision=lax.Precision.HIGHEST
        )
        summed = summed.at[:, first_slot:last_slot].add(contrib)
    return summed * pattern[:, :, None, None].astype(jnp.float32)


def shards(density, pattern):
    masked = density * pattern[:, :, None, None].astype(jnp.float32)
    rim_part = with_halo(masked, ((("row", "depth"), 0),), HALF)
    extended = lax.all_gather(rim_part, "col", axis=2, tiled=True)
    square = banded_local(masked, extended, pattern)
    cube = banded_local(square, extended, pattern)
    return 3.0 * square - 2.0 * cube


def solution(mesh):
    in_specs = (P(("row", "depth"), None, "col", None), P(("row", "depth"), None))
    out_specs = P(("row", "depth"), None, "col", None)
    return jax.shard_map(shards, mesh=mesh, in_specs=in_specs, out_specs=out_specs, check_vma=False)
```

profile of v0, /device:TPU:0, one launch (start us, length us, event | category | flops | bytes accessed | tf_op | source)
XLA Modules:
  0.0 292.7 jit_solution(4097928186245465636)
XLA Ops:
  6.5 0.7 convert_element_type.6
  7.2 2.9 copy_multiply_fusion
  10.2 3.1 %collective-permute-start = (f32[2,5,64,128]{3,2,0,1:T(8,128)S(1)}, f32[2,5,64,128]{3,2,0,1:T(8,128)S(1)}, u32[]{:S(2)}, u32[]{:S(2)}) collective-permute-start(f32[2,5,64,128]{3,2,0,1:T(8,128)S(1)} %get-tuple-element.141), channel_id=1, source_target_pairs={{0,1},{1,2},{2,3},{3,8},{8,9},{9,10},{10,11},{11,16},{16,17},{17,1... | collective-permute-start | bytes 983048 | tf_op jit(solution)/shard_map/ppermute | solution.py:17
  13.3 2.5 collective-permute-start.1
  15.8 7.4 %collective-permute-done = f32[2,5,64,128]{3,2,0,1:T(8,128)S(1)} collective-permute-done((f32[2,5,64,128]{3,2,0,1:T(8,128)S(1)}, f32[2,5,64,128]{3,2,0,1:T(8,128)S(1)}, u32[]{:S(2)}, u32[]{:S(2)}) %collective-permute-start) | collective-permute-done | bytes 327712 | tf_op jit(solution)/shard_map/ppermute | solution.py:17
  23.3 6.3 %collective-permute-done.1 = f32[2,5,64,128]{3,2,0,1:T(8,128)S(1)} collective-permute-done((f32[2,5,64,128]{3,2,0,1:T(8,128)S(1)}, f32[2,5,64,128]{3,2,0,1:T(8,128)S(1)}, u32[]{:S(2)}, u32[]{:S(2)}) %collective-permute-start.1) | collective-permute-done | bytes 327712 | tf_op jit(solution)/shard_map/ppermute | solution.py:19
  29.5 3.0 %pad_maximum_fusion = f32[36,5,64,128]{3,2,0,1:T(8,128)} fusion(f32[2,5,64,128]{3,2,0,1:T(8,128)S(1)} %collective-permute-done.1, f32[32,5,64,128]{3,2,0,1:T(8,128)S(1)} %copy_multiply_fusion, f32[2,5,64,128]{3,2,0,1:T(8,128)S(1)} %collective-permute-done), kind=kLoop, calls=%fused_computation | loop fusion | flops 2949120 | bytes 11796480 | tf_op jit(solution)/shard_map/concatenate | solution.py:15
  32.6 144.0 %all-gather.2.cloned.1.call-done = f32[36,5,128,128]{3,2,0,1:T(8,128)} async-done(((f32[36,5,64,128]{3,2,0,1:T(8,128)}), f32[36,5,128,128]{3,2,0,1:T(8,128)}) %all-gather.2.cloned.1.call-update) | async-done | bytes 11796496 | tf_op jit(solution)/shard_map/all_gather | solution.py:45
  176.5 8.2 %convolution_bitcast_fusion.1 = f32[32,3,64,128]{3,2,0,1:T(8,128)S(1)} fusion(f32[36,5,128,128]{3,2,0,1:T(8,128)} %all-gather.2.cloned.1.call-done, f32[32,5,64,128]{3,2,0,1:T(8,128)} %copy-done.2), kind=kOutput, calls=%fused_computation.17 | convolution fusion | flops 1207959552 | bytes 15990784 | tf_op jit(solution)/shard_map/iab,itbc->itac/dot_general | solution.py:35
  184.8 3.2 %scatter-add.26 = f32[32,5,64,128]{3,2,0,1:T(8,128)} pad(f32[32,3,64,128]{3,2,0,1:T(8,128)S(1)} %convolution_bitcast_fusion.1, f32[]{:T(128)} %constant.250.clone.1), padding=0_0x0_2x0_0x0_0 | pad | bytes 8388612 | tf_op jit(solution)/shard_map/scatter-add | solution.py:38
  188.0 1.1 copy-done.3
  189.1 10.7 %fusion.1 = f32[32,5,64,128]{3,2,0,1:T(8,128)} fusion(f32[32,5,64,128]{3,2,0,1:T(8,128)} %scatter-add.26, f32[36,5,128,128]{3,2,0,1:T(8,128)S(1)} %copy-done, f32[32,5,64,128]{3,2,0,1:T(8,128)S(1)} %copy-done.3), kind=kOutput, calls=%fused_computation.10 | convolution fusion | flops 1611661312 | bytes 21233664 | tf_op jit(solution)/shard_map/iab,itbc->itac/dot_general | solution.py:35
  199.8 12.3 %bitcast_add_fusion.1 = f32[32,5,64,128]{3,2,0,1:T(8,128)S(1)} fusion(f32[32,5,64,128]{3,2,0,1:T(8,128)} %fusion.1, f32[36,5,128,128]{3,2,0,1:T(8,128)S(1)} %copy-done, f32[32,5,64,128]{3,2,0,1:T(8,128)S(1)} %copy-done.3), kind=kOutput, calls=%fused_computation.2 | convolution fusion | flops 2014576640 | bytes 23330816 | tf_op jit(solution)/shard_map/iab,itbc->itac/dot_general | solution.py:35
  212.1 9.5 %constant_dynamic-update-slice_fusion.1 = (f32[32,5,64,128]{3,2,0,1:T(8,128)S(1)}, f32[32,4,64,128]{3,2,0,1:T(8,128)S(1)}) fusion(f32[32,5,64,128]{3,2,0,1:T(8,128)S(1)} %bitcast_add_fusion.1, f32[36,5,128,128]{3,2,0,1:T(8,128)S(1)} %copy-done, f32[32,5,64,128]{3,2,0,1:T(8,128)S(1)} %copy-done.3), kind=kOutput, calls=%fused_computation.29 | convolution fusion | flops 1611661312 | bytes 25427968 | tf_op jit(solution)/shard_map/iab,itbc->itac/dot_general | solution.py:35
  221.6 5.9 %fusion.3 = f32[32,5,64,128]{3,2,0,1:T(8,128)S(1)} fusion(f32[32,5,64,128]{3,2,0,1:T(8,128)S(1)} %get-tuple-element.143, f32[32,4,64,128]{3,2,0,1:T(8,128)S(1)} %get-tuple-element.144, f32[36,5,128,128]{3,2,0,1:T(8,128)S(1)} %copy-done, f32[32,5,64,128]{3,2,0,1:T(8,128)S(1)} %copy-done.3), kind=kOutput, calls=%fused_computation.14 | convolution fusion | flops 1208745984 | bytes 19136512 | tf_op jit(solution)/shard_map/iab,itbc->itac/dot_general | solution.py:35
  227.5 0.6 broadcast_multiply_fusion
  228.1 1.7 copy-done.1
  229.8 5.7 %convolution_bitcast_fusion = f32[32,3,64,128]{3,2,0,1:T(8,128)S(1)} fusion(f32[36,5,128,128]{3,2,0,1:T(8,128)S(1)} %copy-done, f32[32,5,64,128]{3,2,0,1:T(8,128)S(1)} %broadcast_multiply_fusion), kind=kOutput, calls=%fused_computation.16 | convolution fusion | flops 1207959552 | bytes 15990784 | tf_op jit(solution)/shard_map/iab,itbc->itac/dot_general | solution.py:35
  236.0 9.0 %fusion = f32[32,5,64,128]{3,2,0,1:T(8,128)S(1)} fusion(f32[32,5,64,128]{3,2,0,1:T(8,128)S(1)} %scatter-add.34, f32[36,5,128,128]{3,2,0,1:T(8,128)S(1)} %copy-done, f32[32,5,64,128]{3,2,0,1:T(8,128)S(1)} %broadcast_multiply_fusion), kind=kOutput, calls=%fused_computation.8 | convolution fusion | flops 1611661312 | bytes 21233664 | tf_op jit(solution)/shard_map/iab,itbc->itac/dot_general | solution.py:35
  245.1 13.7 %bitcast_add_fusion = f32[32,5,64,128]{3,2,0,1:T(8,128)} fusion(f32[32,5,64,128]{3,2,0,1:T(8,128)S(1)} %fusion, f32[36,5,128,128]{3,2,0,1:T(8,128)S(1)} %copy-done, f32[32,5,64,128]{3,2,0,1:T(8,128)} %copy-done.4), kind=kOutput, calls=%fused_computation.1 | convolution fusion | flops 2014576640 | bytes 23330816 | tf_op jit(solution)/shard_map/iab,itbc->itac/dot_general | solution.py:35
  258.8 11.3 %constant_dynamic-update-slice_fusion = (f32[32,5,64,128]{3,2,0,1:T(8,128)}, f32[32,4,64,128]{3,2,0,1:T(8,128)S(1)}) fusion(f32[32,5,64,128]{3,2,0,1:T(8,128)} %bitcast_add_fusion, f32[36,5,128,128]{3,2,0,1:T(8,128)S(1)} %copy-done, f32[32,5,64,128]{3,2,0,1:T(8,128)} %copy-done.4), kind=kOutput, calls=%fused_computation.28 | convolution fusion | flops 1611661312 | bytes 25427968 | tf_op jit(solution)/shard_map/iab,itbc->itac/dot_general | solution.py:35
  270.1 8.7 %fusion.2 = f32[32,5,64,128]{3,2,0,1:T(8,128)} fusion(f32[32,5,64,128]{3,2,0,1:T(8,128)} %get-tuple-element.145, f32[32,4,64,128]{3,2,0,1:T(8,128)S(1)} %get-tuple-element.146, f32[36,5,128,128]{3,2,0,1:T(8,128)S(1)} %copy-done, f32[32,5,64,128]{3,2,0,1:T(8,128)} %copy-done.4), kind=kOutput, calls=%fused_computation.12 | convolution fusion | flops 1208745984 | bytes 19136512 | tf_op jit(solution)/shard_map/iab,itbc->itac/dot_general | solution.py:35
  278.8 3.6 %multiply_subtract_fusion = f32[32,5,64,128]{3,2,0,1:T(8,128)S(1)} fusion(f32[32,5,64,128]{3,2,0,1:T(8,128)} %fusion.2, f32[32,5]{0,1:T(8,128)S(1)} %copy-done.7, f32[32,5,64,128]{3,2,0,1:T(8,128)S(1)} %bitcast.79), kind=kLoop, calls=%fused_computation.4 | loop fusion | flops 6553600 | bytes 15729280 | tf_op jit(solution)/shard_map/sub | solution.py:48
  282.4 3.0 %copy.24 = f32[32,5,64,128]{3,2,1,0:T(8,128)} copy(f32[32,5,64,128]{3,2,0,1:T(8,128)S(1)} %multiply_subtract_fusion) | data formatting | bytes 10485760 | tf_op jit(solution)/shard_map/sub | solution.py:48
  (23 shorter events, 0.7 us)
Async XLA Ops:
  6.5 170.0 %all-gather.2.cloned.1.call-start = ((), (), s32[]{:S(2)}) async-start(), calls=%async_computation | async-start | bytes 17694720 | tf_op jit(solution)/shard_map/all_gather | solution.py:45
  7.2 2.9 copy-start.5
  10.1 19.4 %copy-start.2 = (f32[32,5,64,128]{3,2,0,1:T(8,128)}, f32[32,5,64,128]{3,2,0,1:T(8,128)S(1)}, u32[]{:S(2)}) copy-start(f32[32,5,64,128]{3,2,0,1:T(8,128)S(1)} %copy_multiply_fusion) | copy-start | bytes 15728644
  10.2 13.0 %collective-permute-start = (f32[2,5,64,128]{3,2,0,1:T(8,128)S(1)}, f32[2,5,64,128]{3,2,0,1:T(8,128)S(1)}, u32[]{:S(2)}, u32[]{:S(2)}) collective-permute-start(f32[2,5,64,128]{3,2,0,1:T(8,128)S(1)} %get-tuple-element.141), channel_id=1, source_target_pairs={{0,1},{1,2},{2,3},{3,8},{8,9},{9,10},{10,11},{11,16},{16,17},{17,1... | collective-permute-start | bytes 983048 | tf_op jit(solution)/shard_map/ppermute | solution.py:17
  13.3 16.2 %collective-permute-start.1 = (f32[2,5,64,128]{3,2,0,1:T(8,128)S(1)}, f32[2,5,64,128]{3,2,0,1:T(8,128)S(1)}, u32[]{:S(2)}, u32[]{:S(2)}) collective-permute-start(f32[2,5,64,128]{3,2,0,1:T(8,128)S(1)} %get-tuple-element.142), channel_id=1, source_target_pairs={{1,0},{2,1},{3,2},{8,3},{9,8},{10,9},{11,10},{16,11},{17,16},{18,1... | collective-permute-start | bytes 983048 | tf_op jit(solution)/shard_map/ppermute | solution.py:19
  176.5 11.4 %copy-start = (f32[36,5,128,128]{3,2,0,1:T(8,128)S(1)}, f32[36,5,128,128]{3,2,0,1:T(8,128)}, u32[]{:S(2)}) copy-start(f32[36,5,128,128]{3,2,0,1:T(8,128)} %all-gather.2.cloned.1.call-done) | copy-start | bytes 35389444
  184.7 4.4 %copy-start.3 = (f32[32,5,64,128]{3,2,0,1:T(8,128)S(1)}, f32[32,5,64,128]{3,2,0,1:T(8,128)}, u32[]{:S(2)}) copy-start(f32[32,5,64,128]{3,2,0,1:T(8,128)} %copy-done.2) | copy-start | bytes 15728644
  221.6 5.9 %copy-start.6 = (f32[32,5]{0,1:T(8,128)S(1)}, f32[32,5]{0,1:T(8,128)}, u32[]{:S(2)}) copy-start(f32[32,5]{0,1:T(8,128)} %copy-done.5) | copy-start | bytes 1924
  227.5 2.3 copy-start.1
  229.8 6.2 %copy-start.4 = (f32[32,5,64,128]{3,2,0,1:T(8,128)}, f32[32,5,64,128]{3,2,0,1:T(8,128)S(1)}, u32[]{:S(2)}) copy-start(f32[32,5,64,128]{3,2,0,1:T(8,128)S(1)} %broadcast_multiply_fusion) | copy-start | bytes 15728644
  245.1 33.7 %slice-start = ((s8[5242880]{0:T(1024)(128)(4,1)}), s8[4194304]{0:T(1024)(128)(4,1)S(1)}, s32[]{:S(2)}) async-start(s8[5242880]{0:T(1024)(128)(4,1)} %bitcast.78), calls=%async_computation.1 | async-start | bytes 8388608
  258.8 20.0 %slice-start.1 = ((s8[5242880]{0:T(1024)(128)(4,1)}), s8[1048576]{0:T(1024)(128)(4,1)S(1)}, s32[]{:S(2)}) async-start(s8[5242880]{0:T(1024)(128)(4,1)} %bitcast.78), calls=%async_computation.2 | async-start | bytes 2097152
  270.1 8.7 %copy-start.7 = (f32[32,5]{0,1:T(8,128)S(1)}, f32[32,5]{0,1:T(8,128)}, u32[]{:S(2)}) copy-start(f32[32,5]{0,1:T(8,128)} %copy-done.5) | copy-start | bytes 1924
Sparse Core Ops, SparseCore 0:
  32.7 143.8 all-gather.1
where the time goes:
time: 299 us; the launch traced here: 293 us
  waiting for transfers between devices  158 us (53%)
  matrix products  94.9 us (32%)
  between operations  14 us (5%)
  other arithmetic  10.8 us (4%)
  local copies, waits for them, and re-layouts  9.76 us (3%)
  starting transfers between devices  5.6 us (2%)
    all_gather x1, waiting for transfers between devices, shards(): extended = lax.all_gather(rim_part, 'col', axis=2, tiled=True)  144 us
    dot_general x10, matrix products, banded_local(): jnp.einsum('iab,itbc->itac', left_tiles[:, source], partner, precision=la...  94.9 us
    ppermute x1, waiting for transfers between devices, with_halo(): lax.ppermute(tail, axis, [(i, (i + 1) % count) for i in range(count)])  7.44 us
    ppermute x1, waiting for transfers between devices, with_halo(): lax.ppermute(head, axis, [((i + 1) % count, i) for i in range(count)])  6.26 us
  transfers between devices with their start and end apart: 3, of which 3 were waited for; matrix products, arithmetic and copies ran while one was open for 0% of the time, Pallas kernels for 0%

commit v1 on v0

v1 whole, which is shorter than its diff:
```python
import functools

import jax
import jax.numpy as jnp
from jax import lax
from jax.experimental import pallas as pl
from jax.experimental.pallas import tpu as pltpu
from jax.sharding import PartitionSpec as P

MESH = pl.DeviceIdType.MESH
WIDE = 5
SLOTS = 6
RING = ("row", "depth")


def split(value):
    high = value.astype(jnp.bfloat16)
    low = (value - high.astype(jnp.float32)).astype(jnp.bfloat16)
    return high, low


def dot(a, b):
    return jnp.dot(a, b, preferred_element_type=jnp.float32)


def kernel(cols, ring, dens, mask, out, raw, masks, high, low, done,
           local_sem, mask_sem, send_sem, recv_sem, edge_send, edge_recv,
           relay_send, relay_recv, mask_send, mask_recv, out_sem):
    pairs = dens.shape[0]
    h = dens.shape[3]
    block = dens.shape[4]
    two = 2 * block
    last = pairs + 1
    me = lax.axis_index("col")
    depth = lax.axis_size("depth")
    place = lax.axis_index("row") * depth + lax.axis_index("depth")

    def on_ring(shift):
        at = lax.rem(place + shift + ring, ring)
        return {"row": at // depth, "depth": lax.rem(at, depth)}

    prev, following = on_ring(-1), on_ring(1)

    def peer(step):
        return {"col": lax.rem(me + step, cols)}

    def source(step):
        return lax.rem(me + cols - step, cols)

    def own(j):
        return pltpu.make_async_copy(dens.at[j - 1], raw.at[me, j], local_sem.at[j - 1])

    def across(step, j):
        return pltpu.make_async_remote_copy(
            dens.at[j - 1], raw.at[me, j], send_sem.at[step - 1, j - 1],
            recv_sem.at[step - 1, j - 1], device_id=peer(step), device_id_type=MESH)

    ends = ((pairs, 0, following), (1, last, prev))

    def edge(side):
        j, slot, device = ends[side]
        return pltpu.make_async_remote_copy(
            dens.at[j - 1], raw.at[me, slot], edge_send.at[side], edge_recv.at[side],
            device_id=device, device_id_type=MESH)

    def relay(side, step):
        j, slot, device = ends[side]
        return pltpu.make_async_remote_copy(
            raw.at[source(step), j], raw.at[source(step), slot], relay_send.at[side, step - 1],
            relay_recv.at[side, step - 1], device_id=device, device_id_type=MESH)

    def mask_edge(side):
        j, slot, device = ends[side]
        return pltpu.make_async_remote_copy(
            mask.at[j - 1], masks.at[slot], mask_send.at[side], mask_recv.at[side],
            device_id=device, device_id_type=MESH)

    def result(j):
        return pltpu.make_async_copy(done.at[j - 1], out.at[j - 1], out_sem.at[j - 1])

    steps = range(1, cols)

    barrier = pltpu.get_barrier_semaphore()
    for device in [peer(s) for s in steps] + [prev, following]:
        pl.semaphore_signal(barrier, inc=1, device_id=device, device_id_type=MESH)
    own_mask = pltpu.make_async_copy(mask, masks.at[pl.ds(1, pairs)], mask_sem)
    own_mask.start()
    pl.semaphore_wait(barrier, cols - 1 + 2)

    for j in (1, pairs):
        for s in steps:
            across(s, j).start()
    for side in (0, 1):
        mask_edge(side).start()
        edge(side).start()

    @pl.loop(2, pairs)
    def _(j):
        for s in steps:
            across(s, j).start()

    @pl.loop(1, pairs + 1)
    def _(j):
        own(j).start()

    def convert(j):
        for p in range(2):
            for s in range(WIDE):
                slot = p + s
                factor = masks[j, p:p + 1, slot * block:(slot + 1) * block]
                for c in range(cols):
                    a, b = split(raw[c, j, p, s] * factor)
                    rows = slice(p * block + c * h, p * block + (c + 1) * h)
                    lanes = slice(slot * block, (slot + 1) * block)
                    high[j, rows, lanes] = a
                    low[j, rows, lanes] = b
            empty = slice(0, block) if p else slice(WIDE * block, SLOTS * block)
            nothing = jnp.zeros((block, block), jnp.bfloat16)
            high[j, p * block:(p + 1) * block, empty] = nothing
            low[j, p * block:(p + 1) * block, empty] = nothing

    def product(j, a, b):
        both = jnp.concatenate([a, b], axis=0)
        m = a.shape[0]
        parts = []
        for n in range(3):
            total = None
            for k in range(3):
                at = n - k + 1
                if at < 0 or at > 2:
                    continue
                lanes = slice(at * two, (at + 1) * two)
                ks = slice(k * two, (k + 1) * two)
                stacked = dot(both[:, ks], high[j + k - 1, :, lanes])
                term = stacked[:m] + stacked[m:] + dot(a[:, ks], low[j + k - 1, :, lanes])
                total = term if total is None else total + term
            parts.append(total)
        return jnp.concatenate(parts, axis=1)

    def compute(j):
        def own_rows(ref):
            return jnp.concatenate(
                [ref[j, pl.ds(pl.multiple_of(p * block + me * h, h), h), :] for p in range(2)], axis=0)

        factor = jnp.concatenate(
            [jnp.broadcast_to(masks[j, p:p + 1, :], (h, SLOTS * block)) for p in range(2)], axis=0)
        square = product(j, own_rows(high), own_rows(low)) * factor
        cube = product(j, *split(square)) * factor
        value = 3.0 * square - 2.0 * cube
        for p in range(2):
            for s in range(WIDE):
                done[j - 1, p, s] = value[p * h:(p + 1) * h, (p + s) * block:(p + s + 1) * block]
        result(j).start()

    own_mask.wait()

    @pl.loop(1, pairs + 1)
    def _(j):
        own(j).wait()

    for j, side in ((1, 1), (pairs, 0)):
        for s in steps:
            across(s, j).wait_recv()
            relay(side, s).start()
        convert(j)
    for side in (0, 1):
        mask_edge(side).wait_recv()
        edge(side).wait_recv()
        for s in steps:
            relay(side, s).wait_recv()
        convert(ends[side][1])

    @pl.loop(2, pairs)
    def _(j):
        for s in steps:
            across(s, j).wait_recv()
        convert(j)
        compute(j - 1)

    @pl.loop(pairs - 1, pairs + 1)
    def _(j):
        compute(j)

    for side in (0, 1):
        mask_edge(side).wait_send()
        edge(side).wait_send()
        for s in steps:
            relay(side, s).wait_send()

    @pl.loop(1, pairs + 1)
    def _(j):
        for s in steps:
            across(s, j).wait_send()
        result(j).wait()


def shards(cols, ring, density, pattern):
    rows, wide, h, block = density.shape
    pairs = rows // 2
    flags = pattern.astype(jnp.float32).reshape(pairs, 2, wide)
    flags = jnp.stack(
        [jnp.pad(flags[:, 0], ((0, 0), (0, 1))), jnp.pad(flags[:, 1], ((0, 0), (1, 0)))], axis=1)
    flags = jnp.pad(flags, ((0, 0), (0, 6), (0, 0)))
    mask = jnp.broadcast_to(flags[..., None], flags.shape + (block,)).reshape(pairs, 8, SLOTS * block)
    paired = density.reshape(pairs, 2, wide, h, block)
    width = SLOTS * block
    dma = pltpu.SemaphoreType.DMA
    out = pl.pallas_call(
        functools.partial(kernel, cols, ring),
        out_shape=jax.ShapeDtypeStruct(paired.shape, jnp.float32),
        in_specs=[pl.BlockSpec(memory_space=pl.ANY)] * 2,
        out_specs=pl.BlockSpec(memory_space=pl.ANY),
        scratch_shapes=[
            pltpu.VMEM((cols, pairs + 2, 2, wide, h, block), jnp.float32),
            pltpu.VMEM((pairs + 2, 8, width), jnp.float32),
            pltpu.VMEM((pairs + 2, 2 * block, width), jnp.bfloat16),
            pltpu.VMEM((pairs + 2, 2 * block, width), jnp.bfloat16),
            pltpu.VMEM(paired.shape, jnp.float32),
            dma((pairs,)),
            dma,
            dma((cols - 1, pairs)),
            dma((cols - 1, pairs)),
            dma((2,)),
            dma((2,)),
            dma((2, cols - 1)),
            dma((2, cols - 1)),
            dma((2,)),
            dma((2,)),
            dma((pairs,)),
        ],
        compiler_params=pltpu.CompilerParams(collective_id=0, has_side_effects=True),
    )(paired, mask)
    return out.reshape(density.shape)


def solution(mesh):
    cols = mesh.shape["col"]
    ring = mesh.shape["row"] * mesh.shape["depth"]
    in_specs = (P(RING, None, "col", None), P(RING, None))
    out_specs = P(RING, None, "col", None)
    body = functools.partial(shards, cols, ring)
    return jax.shard_map(body, mesh=mesh, in_specs=in_specs, out_specs=out_specs, check_vma=False)
```

time: 299 us -> 132 us (0.44); the launches traced: 293 us -> 132 us
  waiting for transfers between devices: 158 us -> 0 us
  Pallas kernels: 0 us -> 124 us
  matrix products: 94.9 us -> 0 us
  between operations: 14 us -> 0.02 us
  other arithmetic: 10.8 us -> 0.7 us
  starting transfers between devices: 5.6 us -> 0 us
    all_gather x1 -> x0, waiting for transfers between devices: 144 us -> none  [shards(): extended = lax.all_gather(rim_part, 'col', axis=2, tiled=True)]
    pallas_call x0 -> x1, Pallas kernels: none -> 124 us  [shards(): pl.pallas_call(functools.partial(kernel, cols, ring), out_shape=jax.Shape...]
    dot_general x10 -> x0, matrix products: 94.9 us -> none  [banded_local(): jnp.einsum('iab,itbc->itac', left_tiles[:, source], partner, precision=la...]
    ppermute x2 -> x0, waiting for transfers between devices: 13.7 us -> none  [the longest x1 7.44 us: with_halo(): lax.ppermute(tail, axis, [(i, (i + 1) % count) for i in range(count)])]
    ppermute x2 -> x0, starting transfers between devices: 5.6 us -> none  [the longest x1 3.11 us: with_halo(): lax.ppermute(tail, axis, [(i, (i + 1) % count) for i in range(count)])]
    scatter-add x2 -> x0, local copies, waits for them, and re-layouts: 3.78 us -> none  [banded_local(): summed = summed.at[:, first_slot:last_slot].add(contrib)]
    sub x1 -> x0, other arithmetic: 3.59 us -> none  [shards(): return 3.0 * square - 2.0 * cube]
    mul x2 -> x0, other arithmetic: 3.48 us -> none  [the longest x1 2.9 us: shards(): masked = density * pattern[:, :, None, None].astype(jnp.float32)]
  transfers between devices with their start and end apart: 3 -> 0, of which waited for: 3 -> 0; matrix products, arithmetic and copies ran while one was open for 0% -> 0% of each run, Pallas kernels for 0% -> 0%
where the time goes in v1:
time: 132 us
  Pallas kernels  124 us (94%)
  local copies, waits for them, and re-layouts  7.03 us (5%)
    pallas_call x1, Pallas kernels, shards(): pl.pallas_call(functools.partial(kernel, cols, ring), out_shape=jax.Shape...  124 us
    unnamed x2, local copies, waits for them, and re-layouts  5.83 us

profile of v1, /device:TPU:0, one launch (start us, length us, event | category | flops | bytes accessed | tf_op | source)
XLA Modules:
  0.0 132.0 jit_solution(6155490442783971819)
XLA Ops:
  0.0 0.7 convert_element_type.9
  0.7 0.1 copy.4
  0.8 0.1 copy.5
  0.9 0.1 copy.6
  1.0 0.1 copy.8
  1.1 0.9 broadcast_bitcast_fusion.mask
  2.0 124.3 %shard_map.28 = f32[16,2,5,64,128]{4,3,2,1,0:T(8,128)} custom-call(f32[16,2,5,64,128]{4,3,2,1,0:T(8,128)} %bitcast.12, f32[16,8,768]{2,1,0:T(8,128)} %broadcast_bitcast_fusion.mask), custom_call_target="tpu_custom_call" | custom-call | tf_op jit(solution)/shard_map/pallas_call | solution.py:208
  126.3 5.7 %copy.10 = f32[32,5,64,128]{3,2,1,0:T(8,128)} copy(f32[32,5,64,128]{3,2,1,0:T(8,128)} %bitcast.11) | data formatting | bytes 10485760
  (4 shorter events, 0.0 us)

commit v2 on v1

--- a/solution.py
+++ b/solution.py
@@ -23,9 +23,9 @@
     return jnp.dot(a, b, preferred_element_type=jnp.float32)
 
 
-def kernel(cols, ring, dens, mask, out, raw, masks, high, low, done,
-           local_sem, mask_sem, send_sem, recv_sem, edge_send, edge_recv,
-           relay_send, relay_recv, mask_send, mask_recv, out_sem):
+def kernel(cols, ring, dens, pattern, out, raw, flags, masks, high, low,
+           local_sem, flag_sem, send_sem, recv_sem, edge_send, edge_recv,
+           relay_send, relay_recv, flag_send, flag_recv):
     pairs = dens.shape[0]
     h = dens.shape[3]
     block = dens.shape[4]
@@ -69,29 +69,25 @@
             raw.at[source(step), j], raw.at[source(step), slot], relay_send.at[side, step - 1],
             relay_recv.at[side, step - 1], device_id=device, device_id_type=MESH)
 
-    def mask_edge(side):
-        j, slot, device = ends[side]
-        return pltpu.make_async_remote_copy(
-            mask.at[j - 1], masks.at[slot], mask_send.at[side], mask_recv.at[side],
-            device_id=device, device_id_type=MESH)
-
-    def result(j):
-        return pltpu.make_async_copy(done.at[j - 1], out.at[j - 1], out_sem.at[j - 1])
+    def flag_edge(side):
+        return pltpu.make_async_remote_copy(
+            pattern, flags.at[2 * side], flag_send.at[side], flag_recv.at[side],
+            device_id=ends[side][2], device_id_type=MESH)
 
     steps = range(1, cols)
 
     barrier = pltpu.get_barrier_semaphore()
     for device in [peer(s) for s in steps] + [prev, following]:
         pl.semaphore_signal(barrier, inc=1, device_id=device, device_id_type=MESH)
-    own_mask = pltpu.make_async_copy(mask, masks.at[pl.ds(1, pairs)], mask_sem)
-    own_mask.start()
+    own_flags = pltpu.make_async_copy(pattern, flags.at[1], flag_sem)
+    own_flags.start()
     pl.semaphore_wait(barrier, cols - 1 + 2)
 
     for j in (1, pairs):
         for s in steps:
             across(s, j).start()
     for side in (0, 1):
-        mask_edge(side).start()
+        flag_edge(side).start()
         edge(side).start()
 
     @pl.loop(2, pairs)
@@ -102,6 +98,16 @@
     @pl.loop(1, pairs + 1)
     def _(j):
         own(j).start()
+
+    def expand(which, i, j):
+        lane = lax.broadcasted_iota(jnp.int32, flags.shape[1:], 1)
+        for p in range(2):
+            picked = jnp.where(lane == i + p, flags[which], 0).astype(jnp.float32)
+            spread = jnp.broadcast_to(jnp.sum(picked, axis=1, keepdims=True), (WIDE, block))
+            for s in range(WIDE):
+                masks[j, p:p + 1, (p + s) * block:(p + s + 1) * block] = spread[s:s + 1]
+            empty = slice(0, block) if p else slice(WIDE * block, SLOTS * block)
+            masks[j, p:p + 1, empty] = jnp.zeros((1, block), jnp.float32)
 
     def convert(j):
         for p in range(2):
@@ -149,10 +155,18 @@
         value = 3.0 * square - 2.0 * cube
         for p in range(2):
             for s in range(WIDE):
-                done[j - 1, p, s] = value[p * h:(p + 1) * h, (p + s) * block:(p + s + 1) * block]
-        result(j).start()
-
-    own_mask.wait()
+                out[j - 1, p, s] = value[p * h:(p + 1) * h, (p + s) * block:(p + s + 1) * block]
+
+    own_flags.wait()
+
+    @pl.loop(1, pairs + 1)
+    def _(j):
+        expand(1, 2 * (j - 1), j)
+
+    for side in (0, 1):
+        flag_edge(side).wait_recv()
+    expand(0, 2 * (pairs - 1), 0)
+    expand(2, 0, last)
 
     @pl.loop(1, pairs + 1)
     def _(j):
@@ -164,7 +178,6 @@
             relay(side, s).start()
         convert(j)
     for side in (0, 1):
-        mask_edge(side).wait_recv()
         edge(side).wait_recv()
         for s in steps:
             relay(side, s).wait_recv()
@@ -182,7 +195,7 @@
         compute(j)
 
     for side in (0, 1):
-        mask_edge(side).wait_send()
+        flag_edge(side).wait_send()
         edge(side).wait_send()
         for s in steps:
             relay(side, s).wait_send()
@@ -191,31 +204,25 @@
     def _(j):
         for s in steps:
             across(s, j).wait_send()
-        result(j).wait()
 
 
 def shards(cols, ring, density, pattern):
     rows, wide, h, block = density.shape
     pairs = rows // 2
-    flags = pattern.astype(jnp.float32).reshape(pairs, 2, wide)
-    flags = jnp.stack(
-        [jnp.pad(flags[:, 0], ((0, 0), (0, 1))), jnp.pad(flags[:, 1], ((0, 0), (1, 0)))], axis=1)
-    flags = jnp.pad(flags, ((0, 0), (0, 6), (0, 0)))
-    mask = jnp.broadcast_to(flags[..., None], flags.shape + (block,)).reshape(pairs, 8, SLOTS * block)
     paired = density.reshape(pairs, 2, wide, h, block)
     width = SLOTS * block
     dma = pltpu.SemaphoreType.DMA
     out = pl.pallas_call(
         functools.partial(kernel, cols, ring),
-        out_shape=jax.ShapeDtypeStruct(paired.shape, jnp.float32),
+        out_shape=pltpu.VMEM(paired.shape, jnp.float32),
         in_specs=[pl.BlockSpec(memory_space=pl.ANY)] * 2,
-        out_specs=pl.BlockSpec(memory_space=pl.ANY),
+        out_specs=pl.BlockSpec(memory_space=pltpu.VMEM),
         scratch_shapes=[
             pltpu.VMEM((cols, pairs + 2, 2, wide, h, block), jnp.float32),
+            pltpu.VMEM((3, wide, rows), jnp.int32),
             pltpu.VMEM((pairs + 2, 8, width), jnp.float32),
             pltpu.VMEM((pairs + 2, 2 * block, width), jnp.bfloat16),
             pltpu.VMEM((pairs + 2, 2 * block, width), jnp.bfloat16),
-            pltpu.VMEM(paired.shape, jnp.float32),
             dma((pairs,)),
             dma,
             dma((cols - 1, pairs)),
@@ -226,10 +233,10 @@
             dma((2, cols - 1)),
             dma((2,)),
             dma((2,)),
-            dma((pairs,)),
         ],
-        compiler_params=pltpu.CompilerParams(collective_id=0, has_side_effects=True),
-    )(paired, mask)
+        compiler_params=pltpu.CompilerParams(
+            collective_id=0, has_side_effects=True, vmem_limit_bytes=48 << 20),
+    )(paired, pattern.T)
     return out.reshape(density.shape)
 
 

time: 132 us -> 127 us (0.962)
  local copies, waits for them, and re-layouts: 7.03 us -> 3.05 us
    unnamed x2 -> x3, local copies, waits for them, and re-layouts: 5.83 us -> 3.05 us
where the time goes in v2:
time: 127 us
  Pallas kernels  124 us (98%)
  local copies, waits for them, and re-layouts  3.05 us (2%)
    pallas_call x1, Pallas kernels, shards(): pl.pallas_call(functools.partial(kernel, cols, ring), out_shape=pltpu.VME...  124 us
    unnamed x3, local copies, waits for them, and re-layouts  3.05 us

profile of v2, /device:TPU:0, one launch (start us, length us, event | category | flops | bytes accessed | tf_op | source)
XLA Modules:
  0.0 126.6 jit_solution(7498736845612507121)
XLA Ops:
  0.0 0.0 copy-start
  0.0 0.7 copy-done
  0.7 123.6 %shard_map.28 = f32[16,2,5,64,128]{4,3,2,1,0:T(8,128)S(1)} custom-call(f32[16,2,5,64,128]{4,3,2,1,0:T(8,128)} %bitcast.5, s32[5,32]{1,0:T(8,128)S(1)} %bitcast.4), custom_call_target="tpu_custom_call" | custom-call | tf_op jit(solution)/shard_map/pallas_call | solution.py:215
  124.3 2.4 %copy.4 = f32[32,5,64,128]{3,2,1,0:T(8,128)} copy(f32[32,5,64,128]{3,2,1,0:T(8,128)S(1)} %bitcast.3) | data formatting | bytes 10485760
Async XLA Ops:
  0.0 0.7 copy-start

commit v3 on v2

v3 whole, which is shorter than its diff:
```python
import functools

import jax
import jax.numpy as jnp
from jax import lax
from jax.experimental import pallas as pl
from jax.experimental.pallas import tpu as pltpu
from jax.sharding import PartitionSpec as P

MESH = pl.DeviceIdType.MESH
WIDE = 5
SLOTS = 6
RING = ("row", "depth")


def split(value):
    high = value.astype(jnp.bfloat16)
    low = (value - high.astype(jnp.float32)).astype(jnp.bfloat16)
    return high, low


def dot(a, b):
    return jnp.dot(a, b, preferred_element_type=jnp.float32)


def products(block, h, me, masks, high, low, out):
    two = 2 * block

    def product(j, a, b):
        both = jnp.concatenate([a, b], axis=0)
        m = a.shape[0]
        parts = []
        for n in range(3):
            total = None
            for k in range(3):
                at = n - k + 1
                if at < 0 or at > 2:
                    continue
                lanes = slice(at * two, (at + 1) * two)
                ks = slice(k * two, (k + 1) * two)
                stacked = dot(both[:, ks], high[j + k - 1, :, lanes])
                term = stacked[:m] + stacked[m:] + dot(a[:, ks], low[j + k - 1, :, lanes])
                total = term if total is None else total + term
            parts.append(total)
        return jnp.concatenate(parts, axis=1)

    def compute(j, to):
        def own_rows(ref):
            return jnp.concatenate(
                [ref[j, pl.ds(pl.multiple_of(p * block + me * h, h), h), :] for p in range(2)], axis=0)

        factor = jnp.concatenate(
            [jnp.broadcast_to(masks[j, p:p + 1, :], (h, SLOTS * block)) for p in range(2)], axis=0)
        square = product(j, own_rows(high), own_rows(low)) * factor
        cube = product(j, *split(square)) * factor
        value = 3.0 * square - 2.0 * cube
        for p in range(2):
            for s in range(WIDE):
                out[to, p, s] = value[p * h:(p + 1) * h, (p + s) * block:(p + s + 1) * block]

    return compute


LATE = 3


def finish(masks, high, low, early, out, late, early_sem, late_sem):
    count, h, block = early.shape[0], early.shape[3], early.shape[4]
    me = lax.axis_index("col")
    first = pltpu.make_async_copy(early, out.at[pl.ds(0, count)], early_sem)
    first.start()
    compute = products(block, h, me, masks, high, low, late)

    def result(i):
        return pltpu.make_async_copy(late.at[i], out.at[count + i], late_sem.at[i])

    @pl.loop(0, LATE)
    def _(i):
        compute(count + 1 + i, i)
        result(i).start()

    first.wait()

    @pl.loop(0, LATE)
    def _(i):
        result(i).wait()


def kernel(cols, ring, dens, pattern, masks, high, low, early, raw, flags,
           local_sem, flag_sem, send_sem, recv_sem, edge_send, edge_recv,
           relay_send, relay_recv, flag_send, flag_recv):
    pairs = dens.shape[0]
    h = dens.shape[3]
    block = dens.shape[4]
    last = pairs + 1
    me = lax.axis_index("col")
    depth = lax.axis_size("depth")
    place = lax.axis_index("row") * depth + lax.axis_index("depth")

    def on_ring(shift):
        at = lax.rem(place + shift + ring, ring)
        return {"row": at // depth, "depth": lax.rem(at, depth)}

    prev, following = on_ring(-1), on_ring(1)

    def peer(step):
        return {"col": lax.rem(me + step, cols)}

    def source(step):
        return lax.rem(me + cols - step, cols)

    def own(j):
        return pltpu.make_async_copy(dens.at[j - 1], raw.at[me, j], local_sem.at[j - 1])

    def across(step, j):
        return pltpu.make_async_remote_copy(
            dens.at[j - 1], raw.at[me, j], send_sem.at[step - 1, j - 1],
            recv_sem.at[step - 1, j - 1], device_id=peer(step), device_id_type=MESH)

    ends = ((pairs, 0, following), (1, last, prev))

    def edge(side):
        j, slot, device = ends[side]
        return pltpu.make_async_remote_copy(
            dens.at[j - 1], raw.at[me, slot], edge_send.at[side], edge_recv.at[side],
            device_id=device, device_id_type=MESH)

    def relay(side, step):
        j, slot, device = ends[side]
        return pltpu.make_async_remote_copy(
            raw.at[source(step), j], raw.at[source(step), slot], relay_send.at[side, step - 1],
            relay_recv.at[side, step - 1], device_id=device, device_id_type=MESH)

    def flag_edge(side):
        return pltpu.make_async_remote_copy(
            pattern, flags.at[2 * side], flag_send.at[side], flag_recv.at[side],
            device_id=ends[side][2], device_id_type=MESH)

    steps = range(1, cols)

    barrier = pltpu.get_barrier_semaphore()
    for device in [peer(s) for s in steps] + [prev, following]:
        pl.semaphore_signal(barrier, inc=1, device_id=device, device_id_type=MESH)
    own_flags = pltpu.make_async_copy(pattern, flags.at[1], flag_sem)
    own_flags.start()
    pl.semaphore_wait(barrier, cols - 1 + 2)

    for j in (1, pairs):
        for s in steps:
            across(s, j).start()
    for side in (0, 1):
        flag_edge(side).start()
        edge(side).start()

    @pl.loop(2, pairs)
    def _(j):
        for s in steps:
            across(s, j).start()

    @pl.loop(1, pairs + 1)
    def _(j):
        own(j).start()

    def expand(which, i, j):
        lane = lax.broadcasted_iota(jnp.int32, flags.shape[1:], 1)
        for p in range(2):
            picked = jnp.where(lane == i + p, flags[which], 0).astype(jnp.float32)
            spread = jnp.broadcast_to(jnp.sum(picked, axis=1, keepdims=True), (WIDE, block))
            for s in range(WIDE):
                masks[j, p:p + 1, (p + s) * block:(p + s + 1) * block] = spread[s:s + 1]
            empty = slice(0, block) if p else slice(WIDE * block, SLOTS * block)
            masks[j, p:p + 1, empty] = jnp.zeros((1, block), jnp.float32)

    def convert(j):
        for p in range(2):
            for s in range(WIDE):
                slot = p + s
                factor = masks[j, p:p + 1, slot * block:(slot + 1) * block]
                for c in range(cols):
                    a, b = split(raw[c, j, p, s] * factor)
                    rows = slice(p * block + c * h, p * block + (c + 1) * h)
                    lanes = slice(slot * block, (slot + 1) * block)
                    high[j, rows, lanes] = a
                    low[j, rows, lanes] = b
            empty = slice(0, block) if p else slice(WIDE * block, SLOTS * block)
            nothing = jnp.zeros((block, block), jnp.bfloat16)
            high[j, p * block:(p + 1) * block, empty] = nothing
            low[j, p * block:(p + 1) * block, empty] = nothing

    compute = products(block, h, me, masks, high, low, early)

    own_flags.wait()

    @pl.loop(1, pairs + 1)
    def _(j):
        expand(1, 2 * (j - 1), j)

    for side in (0, 1):
        flag_edge(side).wait_recv()
    expand(0, 2 * (pairs - 1), 0)
    expand(2, 0, last)

    @pl.loop(1, pairs + 1)
    def _(j):
        own(j).wait()

    for j, side in ((1, 1), (pairs, 0)):
        for s in steps:
            across(s, j).wait_recv()
            relay(side, s).start()
        convert(j)
    for side in (0, 1):
        edge(side).wait_recv()
        for s in steps:
            relay(side, s).wait_recv()
        convert(ends[side][1])

    @pl.loop(2, pairs - 1)
    def _(j):
        for s in steps:
            across(s, j).wait_recv()
        convert(j)
        compute(j - 1, j - 2)

    for side in (0, 1):
        flag_edge(side).wait_send()
        edge(side).wait_send()
        for s in steps:
            relay(side, s).wait_send()
    for s in steps:
        across(s, pairs - 1).wait_recv()
    convert(pairs - 1)

    @pl.loop(1, pairs + 1)
    def _(j):
        for s in steps:
            across(s, j).wait_send()


def shards(cols, ring, density, pattern):
    rows, wide, h, block = density.shape
    pairs = rows // 2
    paired = density.reshape(pairs, 2, wide, h, block)
    width = SLOTS * block
    dma = pltpu.SemaphoreType.DMA
    vmem = pl.BlockSpec(memory_space=pltpu.VMEM)
    held = pl.pallas_call(
        functools.partial(kernel, cols, ring),
        out_shape=[
            pltpu.VMEM((pairs + 2, 8, width), jnp.float32),
            pltpu.VMEM((pairs + 2, 2 * block, width), jnp.bfloat16),
            pltpu.VMEM((pairs + 2, 2 * block, width), jnp.bfloat16),
            pltpu.VMEM((pairs - LATE,) + paired.shape[1:], jnp.float32),
        ],
        in_specs=[pl.BlockSpec(memory_space=pltpu.HBM)] * 2,
        out_specs=[vmem] * 4,
        scratch_shapes=[
            pltpu.VMEM((cols, pairs + 2, 2, wide, h, block), jnp.float32),
            pltpu.VMEM((3, wide, rows), jnp.int32),
            dma((pairs,)),
            dma,
            dma((cols - 1, pairs)),
            dma((cols - 1, pairs)),
            dma((2,)),
            dma((2,)),
            dma((2, cols - 1)),
            dma((2, cols - 1)),
            dma((2,)),
            dma((2,)),
        ],
        compiler_params=pltpu.CompilerParams(
            collective_id=0, has_side_effects=True, vmem_limit_bytes=42 << 20),
    )(*(pltpu.with_memory_space_constraint(x, pltpu.HBM) for x in (paired, pattern.T)))
    out = pl.pallas_call(
        finish,
        out_shape=jax.ShapeDtypeStruct(paired.shape, jnp.float32),
        in_specs=[vmem] * 4,
        out_specs=pl.BlockSpec(memory_space=pltpu.HBM),
        scratch_shapes=[
            pltpu.VMEM((LATE,) + paired.shape[1:], jnp.float32),
            dma,
            dma((LATE,)),
        ],
        compiler_params=pltpu.CompilerParams(vmem_limit_bytes=16 << 20),
    )(*held)
    return out.reshape(density.shape)


def solution(mesh):
    cols = mesh.shape["col"]
    ring = mesh.shape["row"] * mesh.shape["depth"]
    in_specs = (P(RING, None, "col", None), P(RING, None))
    out_specs = P(RING, None, "col", None)
    body = functools.partial(shards, cols, ring)
    return jax.shard_map(body, mesh=mesh, in_specs=in_specs, out_specs=out_specs, check_vma=False)
```

time: 127 us -> 124 us (0.976)
  local copies, waits for them, and re-layouts: 3.05 us -> 0 us
    unnamed x3 -> x0, local copies, waits for them, and re-layouts: 3.05 us -> none
    pallas_call x1 -> x2, Pallas kernels: 124 us -> 124 us  [the longest x1 121 us: shards(): pl.pallas_call(functools.partial(kernel, cols, ring), out_shape=[pltpu.VM...]
where the time goes in v3:
time: 124 us
  Pallas kernels  124 us (100%)
    pallas_call x1, Pallas kernels, shards(): pl.pallas_call(functools.partial(kernel, cols, ring), out_shape=[pltpu.VM...  121 us
    pallas_call x1, Pallas kernels, shards(): pl.pallas_call(finish, out_shape=jax.ShapeDtypeStruct(paired.shape, jnp.f...  3.43 us

profile of v3, /device:TPU:0, one launch (start us, length us, event | category | flops | bytes accessed | tf_op | source)
XLA Modules:
  0.0 124.3 jit_solution(6661180399740721774)
XLA Ops:
  0.0 120.9 %shard_map.28 = (f32[18,8,768]{2,1,0:T(8,128)S(1)}, bf16[18,256,768]{2,1,0:T(8,128)(2,1)S(1)}, bf16[18,256,768]{2,1,0:T(8,128)(2,1)S(1)}, f32[13,2,5,64,128]{4,3,2,1,0:T(8,128)S(1)}) custom-call(f32[16,2,5,64,128]{4,3,2,1,0:T(8,128)} %bitcast.3, s32[5,32]{1,0:T(8,128)} %bitcast.4), custom_call_target="tpu_custom_call" | custom-call | tf_op jit(solution)/shard_map/pallas_call | solution.py:247
  120.9 3.4 %shard_map.29 = f32[16,2,5,64,128]{4,3,2,1,0:T(8,128)} custom-call(f32[18,8,768]{2,1,0:T(8,128)S(1)} %get-tuple-element.9.masks, bf16[18,256,768]{2,1,0:T(8,128)(2,1)S(1)} %get-tuple-element.10.high, bf16[18,256,768]{2,1,0:T(8,128)(2,1)S(1)} %get-tuple-element.11.low, f32[13,2,5,64,128]{4,3,2,1,0:T(8,128)S(1)} %get-tuple-element.12.early), custom_call_target="tpu_custom_call" | custom-call | tf_op jit(solution)/shard_map/pallas_call | solution.py:274

commit v4 on v3

--- a/solution.py
+++ b/solution.py
@@ -88,7 +88,7 @@
 
 def kernel(cols, ring, dens, pattern, masks, high, low, early, raw, flags,
            local_sem, flag_sem, send_sem, recv_sem, edge_send, edge_recv,
-           relay_send, relay_recv, flag_send, flag_recv):
+           relay_send, relay_recv, flag_send, flag_recv, up, down, corner):
     pairs = dens.shape[0]
     h = dens.shape[3]
     block = dens.shape[4]
@@ -138,24 +138,73 @@
 
     steps = range(1, cols)
 
+    z, r = lax.axis_index("depth"), lax.axis_index("row")
+    row_count = lax.axis_size("row")
+
+    def greet(semaphore, device):
+        pl.semaphore_signal(semaphore, inc=1, device_id=device, device_id_type=MESH)
+
+    def along(step):
+        return {"depth": z + step}
+
+    def beside(step):
+        return {"row": lax.rem(r + step + row_count, row_count)}
+
     barrier = pltpu.get_barrier_semaphore()
-    for device in [peer(s) for s in steps] + [prev, following]:
-        pl.semaphore_signal(barrier, inc=1, device_id=device, device_id_type=MESH)
+    for s in steps:
+        greet(barrier, peer(s))
+
+    @pl.when(z > 0)
+    def _():
+        greet(barrier, along(-1))
+
+    @pl.when(z < depth - 1)
+    def _():
+        greet(barrier, along(1))
+
+    @pl.when(z == 0)
+    def _():
+        greet(barrier, beside(-1))
+        greet(barrier, beside(1))
+
     own_flags = pltpu.make_async_copy(pattern, flags.at[1], flag_sem)
     own_flags.start()
-    pl.semaphore_wait(barrier, cols - 1 + 2)
+    near = jnp.where(z == 0, 2, 1) + jnp.where(z < depth - 1, 1, 0)
+    pl.semaphore_wait(barrier, cols - 1 + near)
 
     for j in (1, pairs):
         for s in steps:
             across(s, j).start()
+
+    @pl.loop(2, pairs)
+    def _(j):
+        for s in steps:
+            across(s, j).start()
+
+    @pl.when(z > 0)
+    def _():
+        pl.semaphore_wait(up, 1)
+
+    @pl.when(z < depth - 1)
+    def _():
+        greet(up, along(1))
+
+    @pl.when(z < depth - 2)
+    def _():
+        pl.semaphore_wait(down, 1)
+
+    @pl.when((z > 0) & (z <= depth - 2))
+    def _():
+        greet(down, along(-1))
+
+    @pl.when(z == 0)
+    def _():
+        greet(corner, beside(1))
+        pl.semaphore_wait(corner, 1)
+
     for side in (0, 1):
         flag_edge(side).start()
         edge(side).start()
-
-    @pl.loop(2, pairs)
-    def _(j):
-        for s in steps:
-            across(s, j).start()
 
     @pl.loop(1, pairs + 1)
     def _(j):
@@ -267,6 +316,9 @@
             dma((2, cols - 1)),
             dma((2,)),
             dma((2,)),
+            pltpu.SemaphoreType.REGULAR,
+            pltpu.SemaphoreType.REGULAR,
+            pltpu.SemaphoreType.REGULAR,
         ],
         compiler_params=pltpu.CompilerParams(
             collective_id=0, has_side_effects=True, vmem_limit_bytes=42 << 20),

time: 124 us -> 122 us (0.984)
  Pallas kernels: 124 us -> 122 us
    pallas_call x1, Pallas kernels: 121 us -> 119 us  [shards(): pl.pallas_call(functools.partial(kernel, cols, ring), out_shape=[pltpu.VM...]
where the time goes in v4:
time: 122 us
  Pallas kernels  122 us (100%)
    pallas_call x1, Pallas kernels, shards(): pl.pallas_call(functools.partial(kernel, cols, ring), out_shape=[pltpu.VM...  119 us
    pallas_call x1, Pallas kernels, shards(): pl.pallas_call(finish, out_shape=jax.ShapeDtypeStruct(paired.shape, jnp.f...  3.43 us

profile of v4, /device:TPU:0, one launch (start us, length us, event | category | flops | bytes accessed | tf_op | source)
XLA Modules:
  0.0 122.3 jit_solution(11506737776864888969)
XLA Ops:
  0.0 118.8 %shard_map.28 = (f32[18,8,768]{2,1,0:T(8,128)S(1)}, bf16[18,256,768]{2,1,0:T(8,128)(2,1)S(1)}, bf16[18,256,768]{2,1,0:T(8,128)(2,1)S(1)}, f32[13,2,5,64,128]{4,3,2,1,0:T(8,128)S(1)}) custom-call(f32[16,2,5,64,128]{4,3,2,1,0:T(8,128)} %bitcast.3, s32[5,32]{1,0:T(8,128)} %bitcast.4), custom_call_target="tpu_custom_call" | custom-call | tf_op jit(solution)/shard_map/pallas_call | solution.py:296
  118.8 3.4 %shard_map.29 = f32[16,2,5,64,128]{4,3,2,1,0:T(8,128)} custom-call(f32[18,8,768]{2,1,0:T(8,128)S(1)} %get-tuple-element.9.masks, bf16[18,256,768]{2,1,0:T(8,128)(2,1)S(1)} %get-tuple-element.10.high, bf16[18,256,768]{2,1,0:T(8,128)(2,1)S(1)} %get-tuple-element.11.low, f32[13,2,5,64,128]{4,3,2,1,0:T(8,128)S(1)} %get-tuple-element.12.early), custom_call_target="tpu_custom_call" | custom-call | tf_op jit(solution)/shard_map/pallas_call | solution.py:326

commit v5 on v4

--- a/solution.py
+++ b/solution.py
@@ -26,13 +26,13 @@
 def products(block, h, me, masks, high, low, out):
     two = 2 * block
 
-    def product(j, a, b):
+    def product(j, a, b, sources=(0, 1, 2), start=None):
         both = jnp.concatenate([a, b], axis=0)
         m = a.shape[0]
         parts = []
         for n in range(3):
-            total = None
-            for k in range(3):
+            total = None if start is None else start[:, n * two:(n + 1) * two]
+            for k in sources:
                 at = n - k + 1
                 if at < 0 or at > 2:
                     continue
@@ -44,39 +44,40 @@
             parts.append(total)
         return jnp.concatenate(parts, axis=1)
 
-    def compute(j, to):
-        def own_rows(ref):
-            return jnp.concatenate(
-                [ref[j, pl.ds(pl.multiple_of(p * block + me * h, h), h), :] for p in range(2)], axis=0)
-
+    def own_rows(ref, j):
+        return jnp.concatenate(
+            [ref[j, pl.ds(pl.multiple_of(p * block + me * h, h), h), :] for p in range(2)], axis=0)
+
+    def compute(j, to, sources=(0, 1, 2), start=None):
         factor = jnp.concatenate(
             [jnp.broadcast_to(masks[j, p:p + 1, :], (h, SLOTS * block)) for p in range(2)], axis=0)
-        square = product(j, own_rows(high), own_rows(low)) * factor
+        square = product(j, own_rows(high, j), own_rows(low, j), sources, start) * factor
         cube = product(j, *split(square)) * factor
         value = 3.0 * square - 2.0 * cube
         for p in range(2):
             for s in range(WIDE):
                 out[to, p, s] = value[p * h:(p + 1) * h, (p + s) * block:(p + s + 1) * block]
 
-    return compute
-
-
+    return product, own_rows, compute
+
+
+BEFORE = ((0, 1), (0, 2), (1, 2))
+AFTER = ((2,), (1,), (0,))
 LATE = 3
 
 
-def finish(masks, high, low, early, out, late, early_sem, late_sem):
+def finish(masks, high, low, early, begun, out, late, early_sem, late_sem):
     count, h, block = early.shape[0], early.shape[3], early.shape[4]
     me = lax.axis_index("col")
     first = pltpu.make_async_copy(early, out.at[pl.ds(0, count)], early_sem)
     first.start()
-    compute = products(block, h, me, masks, high, low, late)
+    _, _, compute = products(block, h, me, masks, high, low, late)
 
     def result(i):
         return pltpu.make_async_copy(late.at[i], out.at[count + i], late_sem.at[i])
 
-    @pl.loop(0, LATE)
-    def _(i):
-        compute(count + 1 + i, i)
+    for i in range(LATE):
+        compute(count + 1 + i, i, AFTER[i], begun[i])
         result(i).start()
 
     first.wait()
@@ -86,7 +87,7 @@
         result(i).wait()
 
 
-def kernel(cols, ring, dens, pattern, masks, high, low, early, raw, flags,
+def kernel(cols, ring, dens, pattern, masks, high, low, early, begun, raw, flags,
            local_sem, flag_sem, send_sem, recv_sem, edge_send, edge_recv,
            relay_send, relay_recv, flag_send, flag_recv, up, down, corner):
     pairs = dens.shape[0]
@@ -236,7 +237,7 @@
             high[j, p * block:(p + 1) * block, empty] = nothing
             low[j, p * block:(p + 1) * block, empty] = nothing
 
-    compute = products(block, h, me, masks, high, low, early)
+    product, own_rows, compute = products(block, h, me, masks, high, low, early)
 
     own_flags.wait()
 
@@ -270,6 +271,20 @@
             across(s, j).wait_recv()
         convert(j)
         compute(j - 1, j - 2)
+
+    def local_rows(j):
+        rows = []
+        for p in range(2):
+            blocks = [raw[me, j, p, s] for s in range(WIDE)]
+            empty = [jnp.zeros((h, block), jnp.float32)]
+            row = jnp.concatenate(empty + blocks if p else blocks + empty, axis=1)
+            rows.append(row * masks[j, p:p + 1, :])
+        return split(jnp.concatenate(rows, axis=0))
+
+    for i in range(LATE):
+        j = pairs - LATE + 1 + i
+        a, b = local_rows(j) if i == 1 else (own_rows(high, j), own_rows(low, j))
+        begun[i] = product(j, a, b, BEFORE[i])
 
     for side in (0, 1):
         flag_edge(side).wait_send()
@@ -300,9 +315,10 @@
             pltpu.VMEM((pairs + 2, 2 * block, width), jnp.bfloat16),
             pltpu.VMEM((pairs + 2, 2 * block, width), jnp.bfloat16),
             pltpu.VMEM((pairs - LATE,) + paired.shape[1:], jnp.float32),
+            pltpu.VMEM((LATE, 2 * h, width), jnp.float32),
         ],
         in_specs=[pl.BlockSpec(memory_space=pltpu.HBM)] * 2,
-        out_specs=[vmem] * 4,
+        out_specs=[vmem] * 5,
         scratch_shapes=[
             pltpu.VMEM((cols, pairs + 2, 2, wide, h, block), jnp.float32),
             pltpu.VMEM((3, wide, rows), jnp.int32),
@@ -326,7 +342,7 @@
     out = pl.pallas_call(
         finish,
         out_shape=jax.ShapeDtypeStruct(paired.shape, jnp.float32),
-        in_specs=[vmem] * 4,
+        in_specs=[vmem] * 5,
         out_specs=pl.BlockSpec(memory_space=pltpu.HBM),
         scratch_shapes=[
             pltpu.VMEM((LATE,) + paired.shape[1:], jnp.float32),

time: 122 us -> 121 us (level)
  no operation moved by 1% of the time
where the time goes in v5:
time: 121 us
  Pallas kernels  121 us (100%)
    pallas_call x1, Pallas kernels, shards(): pl.pallas_call(functools.partial(kernel, cols, ring), out_shape=[pltpu.VM...  119 us
    pallas_call x1, Pallas kernels, shards(): pl.pallas_call(finish, out_shape=jax.ShapeDtypeStruct(paired.shape, jnp.f...  2.46 us

profile of v5, /device:TPU:0, one launch (start us, length us, event | category | flops | bytes accessed | tf_op | source)
XLA Modules:
  0.0 121.3 jit_solution(555815792851718887)
XLA Ops:
  0.0 118.8 %shard_map.28 = (f32[18,8,768]{2,1,0:T(8,128)S(1)}, bf16[18,256,768]{2,1,0:T(8,128)(2,1)S(1)}, bf16[18,256,768]{2,1,0:T(8,128)(2,1)S(1)}, f32[13,2,5,64,128]{4,3,2,1,0:T(8,128)S(1)}, f32[3,128,768]{2,1,0:T(8,128)S(1)}) custom-call(f32[16,2,5,64,128]{4,3,2,1,0:T(8,128)} %bitcast.3, s32[5,32]{1,0:T(8,128)} %bitcast.4), custom_call_target="tpu_custom_call" | custom-call | tf_op jit(solution)/shard_map/pallas_call | solution.py:311
  118.8 2.5 %shard_map.29 = f32[16,2,5,64,128]{4,3,2,1,0:T(8,128)} custom-call(f32[18,8,768]{2,1,0:T(8,128)S(1)} %get-tuple-element.10.masks, bf16[18,256,768]{2,1,0:T(8,128)(2,1)S(1)} %get-tuple-element.11.high, bf16[18,256,768]{2,1,0:T(8,128)(2,1)S(1)} %get-tuple-element.12.low, f32[13,2,5,64,128]{4,3,2,1,0:T(8,128)S(1)} %get-tuple-element.13.early, ...), custom_call_target="tpu_custom_call" | custom-call | tf_op jit(solution)/shard_map/pallas_call | solution.py:342

commit v6 on v5

--- a/solution.py
+++ b/solution.py
@@ -69,8 +69,11 @@
 def finish(masks, high, low, early, begun, out, late, early_sem, late_sem):
     count, h, block = early.shape[0], early.shape[3], early.shape[4]
     me = lax.axis_index("col")
-    first = pltpu.make_async_copy(early, out.at[pl.ds(0, count)], early_sem)
-    first.start()
+    def ready(i):
+        return pltpu.make_async_copy(early.at[i], out.at[i], early_sem.at[i])
+
+    for i in range(count):
+        ready(i).start()
     _, _, compute = products(block, h, me, masks, high, low, late)
 
     def result(i):
@@ -80,7 +83,8 @@
         compute(count + 1 + i, i, AFTER[i], begun[i])
         result(i).start()
 
-    first.wait()
+    for i in range(count):
+        ready(i).wait()
 
     @pl.loop(0, LATE)
     def _(i):
@@ -346,7 +350,7 @@
         out_specs=pl.BlockSpec(memory_space=pltpu.HBM),
         scratch_shapes=[
             pltpu.VMEM((LATE,) + paired.shape[1:], jnp.float32),
-            dma,
+            dma((pairs - LATE,)),
             dma((LATE,)),
         ],
         compiler_params=pltpu.CompilerParams(vmem_limit_bytes=16 << 20),

time: 121 us -> 122 us (level)
  no operation moved by 1% of the time
where the time goes in v6:
time: 122 us; the launch traced here: 121 us
  Pallas kernels  121 us (99%)
    pallas_call x1, Pallas kernels, shards(): pl.pallas_call(functools.partial(kernel, cols, ring), out_shape=[pltpu.VM...  119 us
    pallas_call x1, Pallas kernels, shards(): pl.pallas_call(finish, out_shape=jax.ShapeDtypeStruct(paired.shape, jnp.f...  2.57 us

profile of v6, /device:TPU:0, one launch (start us, length us, event | category | flops | bytes accessed | tf_op | source)
XLA Modules:
  0.0 121.4 jit_solution(12420686343964697139)
XLA Ops:
  0.0 118.8 %shard_map.28 = (f32[18,8,768]{2,1,0:T(8,128)S(1)}, bf16[18,256,768]{2,1,0:T(8,128)(2,1)S(1)}, bf16[18,256,768]{2,1,0:T(8,128)(2,1)S(1)}, f32[13,2,5,64,128]{4,3,2,1,0:T(8,128)S(1)}, f32[3,128,768]{2,1,0:T(8,128)S(1)}) custom-call(f32[16,2,5,64,128]{4,3,2,1,0:T(8,128)} %bitcast.3, s32[5,32]{1,0:T(8,128)} %bitcast.4), custom_call_target="tpu_custom_call" | custom-call | tf_op jit(solution)/shard_map/pallas_call | solution.py:315
  118.8 2.6 %shard_map.29 = f32[16,2,5,64,128]{4,3,2,1,0:T(8,128)} custom-call(f32[18,8,768]{2,1,0:T(8,128)S(1)} %get-tuple-element.10.masks, bf16[18,256,768]{2,1,0:T(8,128)(2,1)S(1)} %get-tuple-element.11.high, bf16[18,256,768]{2,1,0:T(8,128)(2,1)S(1)} %get-tuple-element.12.low, f32[13,2,5,64,128]{4,3,2,1,0:T(8,128)S(1)} %get-tuple-element.13.early, ...), custom_call_target="tpu_custom_call" | custom-call | tf_op jit(solution)/shard_map/pallas_call | solution.py:346
